TPU v7x, 256 devices: a whole 4x4x8 slice. The times are simulated.
256 devices in a mesh: lx: 8 (over z), ly: 8 (over x, y_lo), blk: 4 (over y_hi, core).
Axes of the slice: x: 4, y: 4 (y_hi: 2, y_lo: 2; y = y_hi * 2 + y_lo), z: 8, core: 2. Of those that a mesh axis runs over, the one named last changes fastest.
Arguments:
- block_vectors: float32 [32, 1024, 2048], P('blk', 'lx', 'ly'), may hold values from -6 to 6
- search_vectors: float32 [256, 1024, 2048], P('blk', 'lx', 'ly'), may hold values from -6 to 6
- onsite_energy: float32 [1024, 2048], P('lx', 'ly'), may hold values from -1 to 1
- site_mask: int32 [1024, 2048], P('lx', 'ly'), may hold values 0 or 1
- filter_coefs: float32 [5], replicated, may hold values from -1 to 1
Outputs:
- projected: float32 [2, 32, 256], P(None, None, 'blk')
Inputs may be any that keep to these rules, and one draw needn't show every extreme that they name: `site_mask`: 1 marks a present site, 0 a vacancy.
All inputs are finite; a program needn't handle non-finite values. No bound on the sum of `site_mask` on one device may be relied on, other than what follows from the above.
Results may differ from a plain program's by a relative error of at most 0.00016.
Values sent between devices are 32-bit elements; how exact they have to be, the bound alone decides.
No kernel may reach another device: no remote copies, remote signals or barrier semaphores. Data moves between devices by JAX's collectives and lax.ppermute only.
A program may use at most 64 MiB of HBM per device.

v0:
```python
import math
import jax
import jax.numpy as jnp
from jax import lax
from jax.sharding import PartitionSpec as P


def extended(block, sides, width):
    for axis, dim in sides:
        count = lax.axis_size(axis)
        forward = [(i, i + 1) for i in range(count - 1)]
        backward = [(target, source) for source, target in forward]
        low = lax.ppermute(
            lax.slice_in_dim(block, block.shape[dim] - width, None, axis=dim), axis, forward
        )
        high = lax.ppermute(lax.slice_in_dim(block, 0, width, axis=dim), axis, backward)
        block = jnp.concatenate([low, block, high], axis=dim)
    return block


def scaled_step(padded, onsite, present):
    nrows, ncols = onsite.shape
    row_index = lax.broadcasted_iota(jnp.int32, (nrows, ncols), 0)
    col_index = lax.broadcasted_iota(jnp.int32, (nrows, ncols), 1)
    even_sites = (row_index + col_index) % 2 == 0
    centre = padded[..., 1:-1, 1:-1]
    left_side = padded[..., 1:-1, :-2]
    right_side = padded[..., 1:-1, 2:]
    upper_side = padded[..., :-2, 1:-1]
    lower_side = padded[..., 2:, 1:-1]
    vertical = jnp.where(even_sites, lower_side, upper_side)
    return present * (onsite * centre - (left_side + right_side + vertical)) * 0.25


def gram_rows(stacked, search_vectors):
    stacks, members, nrows, ncols = stacked.shape
    flat = stacked.reshape(stacks * members, nrows * ncols)
    search_flat = search_vectors.reshape(search_vectors.shape[0], nrows * ncols)
    result = lax.dot_general(
        flat,
        search_flat,
        (((1,), (1,)), ((), ())),
        precision=lax.Precision.HIGHEST,
        preferred_element_type=jnp.float32,
    )
    return result.reshape(stacks, members, search_vectors.shape[0])


def shards(block_vectors, search_vectors, onsite_energy, site_mask, filter_coefs):
    present = site_mask.astype(jnp.float32)
    current = block_vectors * present
    filtered = filter_coefs[0] * current
    degree = filter_coefs.shape[0] - 1
    before = current
    for order in range(1, degree + 1):
        padded_field = extended(current, (("lx", 1), ("ly", 2)), 1)
        image = scaled_step(padded_field, onsite_energy, present)
        following = image if order == 1 else 2.0 * image - before
        before, current = (current, following)
        filtered = filtered + filter_coefs[order] * current
    nrows, ncols = onsite_energy.shape
    scale_factor = 1.0 / math.sqrt(nrows * ncols * lax.axis_size("lx") * lax.axis_size("ly"))
    padded_field = extended(filtered, (("lx", 1), ("ly", 2)), 1)
    image = scaled_step(padded_field, onsite_energy, present)
    paired = jnp.stack([filtered, image])
    partial_gram = gram_rows(lax.all_gather(paired, "blk", axis=1, tiled=True), search_vectors)
    total = lax.psum(partial_gram, ("lx", "ly"))
    return total * scale_factor


def solution(mesh):
    placed = (P("blk", "lx", "ly"), P("blk", "lx", "ly"), P("lx", "ly"), P("lx", "ly"), P())
    return jax.shard_map(
        shards, mesh=mesh, in_specs=placed, out_specs=P(None, None, "blk"), check_vma=False
    )
```

profile of v0, /device:TPU:16, one launch (start us, length us, event | category | flops | bytes accessed | tf_op | source)
XLA Modules:
  0.0 537.4 jit_solution(5126460402475514423)
XLA Ops:
  7.5 1.8 copy_multiply_fusion
  9.3 1.3 collective-permute-start.1
  10.6 4.5 collective-permute-start
  15.2 1.3 collective-permute-done
  17.5 1.3 collective-permute-start.3
  18.8 4.5 collective-permute-start.2
  23.4 1.3 collective-permute-done.2
  24.7 1.2 copy.10
  25.9 1.2 copy.12
  27.1 1.9 broadcast_multiply_fusion
  29.0 1.3 collective-permute-start.5
  30.3 4.8 collective-permute-start.4
  35.2 1.3 collective-permute-done.4
  37.6 1.4 copy.13
  39.3 1.3 collective-permute-start.7
  40.6 4.8 collective-permute-start.6
  46.8 1.2 copy.14
  48.0 1.2 copy.16
  49.2 2.6 fusion.34
  51.8 1.3 collective-permute-start.9
  53.1 4.8 collective-permute-start.8
  58.0 1.3 collective-permute-done.8
  60.4 1.4 copy.17
  61.8 5.0 collective-permute-start.10
  67.1 1.3 collective-permute-start.11
  68.8 5.0 collective-permute-done.11
  73.8 1.2 copy.20
  75.0 1.8 fusion.27
  76.8 1.3 collective-permute-start.13
  78.1 4.9 collective-permute-start.12
  83.1 1.3 collective-permute-done.12
  85.5 1.4 copy.21
  87.2 1.3 collective-permute-start.15
  88.5 5.4 %collective-permute-start.14 = (f32[8,130,1]{1,0,2:T(8,128)S(1)}, f32[8,130,1]{1,0,2:T(8,128)S(1)}, u32[]{:S(2)}, u32[]{:S(2)}) collective-permute-start(f32[8,130,1]{1,0,2:T(8,128)S(1)} %copy.21), channel_id=1, source_target_pairs={{0,4},{4,8},{8,12},{12,16},{16,20},{20,24},{24,28},{1,5},{5,9},{9,... | collective-permute-start | bytes 12488 | tf_op jit(solution)/shard_map/ppermute | solution.py:13
  95.3 1.2 copy.22
  97.7 8.3 %fusion.20 = f32[8,128,256]{2,0,1:T(8,128)S(1)} fusion(f32[8,128,256]{2,0,1:T(8,128)S(1)} %fusion.34, f32[8,128,256]{2,0,1:T(8,128)} %copy-done, f32[8,1,256]{2,0,1:T(8,128)S(1)} %collective-permute-done.12, f32[8,1,256]{2,0,1:T(8,128)S(1)} %collective-permute-done.13, f32[8,130,1]{2,0,1:T(8,128)} %copy.24, f32[8,130,1]{2,0,1:T(8,128)} %copy.22, ...), kind=kLoop, calls=%fused_computation.33 | loop fusion | flops 6815744 | bytes 5562516 | tf_op jit(solution)/shard_map/add | solution.py:60
  106.0 1.3 collective-permute-start.17
  107.3 6.0 %collective-permute-start.16 = (f32[8,1,256]{2,0,1:T(8,128)S(1)}, f32[8,1,256]{2,0,1:T(8,128)S(1)}, u32[]{:S(2)}, u32[]{:S(2)}) collective-permute-start(f32[8,1,256]{2,0,1:T(8,128)S(1)} %get-tuple-element.18), channel_id=1, source_target_pairs={{0,32},{32,64},{64,96},{96,128},{128,160},{160,192},{192,224},{1,3... | collective-permute-start | bytes 24584 | tf_op jit(solution)/shard_map/ppermute | solution.py:13
  113.3 1.3 collective-permute-done.16
  115.3 4.8 collective-permute-start.18
  120.5 1.5 collective-permute-start.19
  122.4 4.8 collective-permute-done.19
  127.2 1.2 copy.28
  128.4 1.8 fusion.11
  130.2 1.5 pad_maximum_fusion
  131.7 71.7 %all-gather.2.cloned.1.call-done = f32[2,32,128,256]{3,1,2,0:T(8,128)} async-done(((f32[2,8,128,256]{3,1,2,0:T(8,128)}), f32[2,32,128,256]{3,1,2,0:T(8,128)}) %all-gather.2.cloned.1.call-update) | async-done | bytes 8388624 | tf_op jit(solution)/shard_map/all_gather | solution.py:66
  203.4 16.7 %fusion.3 = f32[2,32,64]{2,1,0:T(8,128)S(1)} fusion(f32[2,32,128,256]{3,1,2,0:T(8,128)} %all-gather.2.cloned.1.call-done, f32[64,128,256]{2,1,0:T(8,128)} %param.6), kind=kOutput, calls=%fused_computation.4 | convolution fusion | flops 1610612736 | bytes 16793600 | tf_op jit(solution)/shard_map/dot_general | solution.py:39
  220.0 309.9 %psum.7 = f32[2,32,64]{2,1,0:T(8,128)S(1)} all-reduce(f32[2,32,64]{2,1,0:T(8,128)S(1)} %fusion.3), channel_id=1, replica_groups=mesh['lx'=8,'ly'=8,'blk'=4] {'lx','ly'}, use_global_device_ids=true, to_apply=%region_0.1 | all-reduce | flops 4096 | bytes 32768 | tf_op jit(solution)/shard_map/psum | solution.py:67
  (50 shorter events, 12.0 us)
Async XLA Ops:
  6.5 196.8 %all-gather.2.cloned.1.call-start = ((), (), s32[]{:S(2)}) async-start(), calls=%async_computation | async-start | bytes 10485760 | tf_op jit(solution)/shard_map/all_gather | solution.py:66
  9.3 5.9 %collective-permute-start.1 = (f32[8,1,256]{2,0,1:T(8,128)S(1)}, f32[8,1,256]{2,0,1:T(8,128)S(1)}, u32[]{:S(2)}, u32[]{:S(2)}) collective-permute-start(f32[8,1,256]{2,0,1:T(8,128)S(1)} %get-tuple-element.25), channel_id=1, source_target_pairs={{32,0},{64,32},{96,64},{128,96},{160,128},{192,160},{224,192},{33,... | collective-permute-start | bytes 24584 | tf_op jit(solution)/shard_map/ppermute | solution.py:16
  10.6 5.9 %collective-permute-start = (f32[8,1,256]{2,0,1:T(8,128)S(1)}, f32[8,1,256]{2,0,1:T(8,128)S(1)}, u32[]{:S(2)}, u32[]{:S(2)}) collective-permute-start(f32[8,1,256]{2,0,1:T(8,128)S(1)} %get-tuple-element.26), channel_id=1, source_target_pairs={{0,32},{32,64},{64,96},{96,128},{128,160},{160,192},{192,224},{1,3... | collective-permute-start | bytes 24584 | tf_op jit(solution)/shard_map/ppermute | solution.py:13
  16.8 10.3 %copy-start.1 = (f32[128,256]{1,0:T(8,128)S(1)}, f32[128,256]{1,0:T(8,128)}, u32[]{:S(2)}) copy-start(f32[128,256]{1,0:T(8,128)} %param.7) | copy-start | bytes 393220
  17.5 8.4 %collective-permute-start.3 = (f32[8,130,1]{1,0,2:T(8,128)S(1)}, f32[8,130,1]{1,0,2:T(8,128)S(1)}, u32[]{:S(2)}, u32[]{:S(2)}) collective-permute-start(f32[8,130,1]{1,0,2:T(8,128)S(1)} %copy.11), channel_id=1, source_target_pairs={{4,0},{8,4},{12,8},{16,12},{20,16},{24,20},{28,24},{5,1},{9,5},{13... | collective-permute-start | bytes 12488 | tf_op jit(solution)/shard_map/ppermute | solution.py:16
  18.8 5.9 %collective-permute-start.2 = (f32[8,130,1]{1,0,2:T(8,128)S(1)}, f32[8,130,1]{1,0,2:T(8,128)S(1)}, u32[]{:S(2)}, u32[]{:S(2)}) collective-permute-start(f32[8,130,1]{1,0,2:T(8,128)S(1)} %copy.9), channel_id=1, source_target_pairs={{0,4},{4,8},{8,12},{12,16},{16,20},{20,24},{24,28},{1,5},{5,9},{9,... | collective-permute-start | bytes 12488 | tf_op jit(solution)/shard_map/ppermute | solution.py:13
  29.0 6.1 %collective-permute-start.5 = (f32[8,1,256]{2,0,1:T(8,128)S(1)}, f32[8,1,256]{2,0,1:T(8,128)S(1)}, u32[]{:S(2)}, u32[]{:S(2)}) collective-permute-start(f32[8,1,256]{2,0,1:T(8,128)S(1)} %get-tuple-element.23), channel_id=1, source_target_pairs={{32,0},{64,32},{96,64},{128,96},{160,128},{192,160},{224,192},{33,... | collective-permute-start | bytes 24584 | tf_op jit(solution)/shard_map/ppermute | solution.py:16
  30.3 6.2 %collective-permute-start.4 = (f32[8,1,256]{2,0,1:T(8,128)S(1)}, f32[8,1,256]{2,0,1:T(8,128)S(1)}, u32[]{:S(2)}, u32[]{:S(2)}) collective-permute-start(f32[8,1,256]{2,0,1:T(8,128)S(1)} %get-tuple-element.24), channel_id=1, source_target_pairs={{0,32},{32,64},{64,96},{96,128},{128,160},{160,192},{192,224},{1,3... | collective-permute-start | bytes 24584 | tf_op jit(solution)/shard_map/ppermute | solution.py:13
  39.3 8.7 %collective-permute-start.7 = (f32[8,130,1]{1,0,2:T(8,128)S(1)}, f32[8,130,1]{1,0,2:T(8,128)S(1)}, u32[]{:S(2)}, u32[]{:S(2)}) collective-permute-start(f32[8,130,1]{1,0,2:T(8,128)S(1)} %copy.15), channel_id=1, source_target_pairs={{4,0},{8,4},{12,8},{16,12},{20,16},{24,20},{28,24},{5,1},{9,5},{13... | collective-permute-start | bytes 12488 | tf_op jit(solution)/shard_map/ppermute | solution.py:16
  40.6 6.2 %collective-permute-start.6 = (f32[8,130,1]{1,0,2:T(8,128)S(1)}, f32[8,130,1]{1,0,2:T(8,128)S(1)}, u32[]{:S(2)}, u32[]{:S(2)}) collective-permute-start(f32[8,130,1]{1,0,2:T(8,128)S(1)} %copy.13), channel_id=1, source_target_pairs={{0,4},{4,8},{8,12},{12,16},{16,20},{20,24},{24,28},{1,5},{5,9},{9,... | collective-permute-start | bytes 12488 | tf_op jit(solution)/shard_map/ppermute | solution.py:13
  51.8 6.1 %collective-permute-start.9 = (f32[8,1,256]{2,0,1:T(8,128)S(1)}, f32[8,1,256]{2,0,1:T(8,128)S(1)}, u32[]{:S(2)}, u32[]{:S(2)}) collective-permute-start(f32[8,1,256]{2,0,1:T(8,128)S(1)} %get-tuple-element.21), channel_id=1, source_target_pairs={{32,0},{64,32},{96,64},{128,96},{160,128},{192,160},{224,192},{33,... | collective-permute-start | bytes 24584 | tf_op jit(solution)/shard_map/ppermute | solution.py:16
  53.1 6.2 %collective-permute-start.8 = (f32[8,1,256]{2,0,1:T(8,128)S(1)}, f32[8,1,256]{2,0,1:T(8,128)S(1)}, u32[]{:S(2)}, u32[]{:S(2)}) collective-permute-start(f32[8,1,256]{2,0,1:T(8,128)S(1)} %get-tuple-element.22), channel_id=1, source_target_pairs={{0,32},{32,64},{64,96},{96,128},{128,160},{160,192},{192,224},{1,3... | collective-permute-start | bytes 24584 | tf_op jit(solution)/shard_map/ppermute | solution.py:13
  61.8 6.6 %collective-permute-start.10 = (f32[8,130,1]{1,0,2:T(8,128)S(1)}, f32[8,130,1]{1,0,2:T(8,128)S(1)}, u32[]{:S(2)}, u32[]{:S(2)}) collective-permute-start(f32[8,130,1]{1,0,2:T(8,128)S(1)} %copy.17), channel_id=1, source_target_pairs={{0,4},{4,8},{8,12},{12,16},{16,20},{20,24},{24,28},{1,5},{5,9},{9,... | collective-permute-start | bytes 12488 | tf_op jit(solution)/shard_map/ppermute | solution.py:13
  67.1 6.7 %collective-permute-start.11 = (f32[8,130,1]{1,0,2:T(8,128)S(1)}, f32[8,130,1]{1,0,2:T(8,128)S(1)}, u32[]{:S(2)}, u32[]{:S(2)}) collective-permute-start(f32[8,130,1]{1,0,2:T(8,128)S(1)} %copy.19), channel_id=1, source_target_pairs={{4,0},{8,4},{12,8},{16,12},{20,16},{24,20},{28,24},{5,1},{9,5},{13... | collective-permute-start | bytes 12488 | tf_op jit(solution)/shard_map/ppermute | solution.py:16
  76.8 7.7 %copy-start = (f32[8,128,256]{2,0,1:T(8,128)}, f32[8,128,256]{2,0,1:T(8,128)S(1)}, u32[]{:S(2)}) copy-start(f32[8,128,256]{2,0,1:T(8,128)S(1)} %fusion.27) | copy-start | bytes 3145732
  76.8 6.2 %collective-permute-start.13 = (f32[8,1,256]{2,0,1:T(8,128)S(1)}, f32[8,1,256]{2,0,1:T(8,128)S(1)}, u32[]{:S(2)}, u32[]{:S(2)}) collective-permute-start(f32[8,1,256]{2,0,1:T(8,128)S(1)} %get-tuple-element.19), channel_id=1, source_target_pairs={{32,0},{64,32},{96,64},{128,96},{160,128},{192,160},{224,192},{33,... | collective-permute-start | bytes 24584 | tf_op jit(solution)/shard_map/ppermute | solution.py:16
  78.1 6.3 %collective-permute-start.12 = (f32[8,1,256]{2,0,1:T(8,128)S(1)}, f32[8,1,256]{2,0,1:T(8,128)S(1)}, u32[]{:S(2)}, u32[]{:S(2)}) collective-permute-start(f32[8,1,256]{2,0,1:T(8,128)S(1)} %get-tuple-element.20), channel_id=1, source_target_pairs={{0,32},{32,64},{64,96},{96,128},{128,160},{160,192},{192,224},{1,3... | collective-permute-start | bytes 24584 | tf_op jit(solution)/shard_map/ppermute | solution.py:13
  85.5 8.5 %copy-start.2 = (f32[5]{0:T(128)S(1)}, f32[5]{0:T(128)}, u32[]{:S(2)}) copy-start(f32[5]{0:T(128)} %param.9) | copy-start | bytes 64
  87.2 9.3 %collective-permute-start.15 = (f32[8,130,1]{1,0,2:T(8,128)S(1)}, f32[8,130,1]{1,0,2:T(8,128)S(1)}, u32[]{:S(2)}, u32[]{:S(2)}) collective-permute-start(f32[8,130,1]{1,0,2:T(8,128)S(1)} %copy.23), channel_id=1, source_target_pairs={{4,0},{8,4},{12,8},{16,12},{20,16},{24,20},{28,24},{5,1},{9,5},{13... | collective-permute-start | bytes 12488 | tf_op jit(solution)/shard_map/ppermute | solution.py:16
  88.5 6.8 %collective-permute-start.14 = (f32[8,130,1]{1,0,2:T(8,128)S(1)}, f32[8,130,1]{1,0,2:T(8,128)S(1)}, u32[]{:S(2)}, u32[]{:S(2)}) collective-permute-start(f32[8,130,1]{1,0,2:T(8,128)S(1)} %copy.21), channel_id=1, source_target_pairs={{0,4},{4,8},{8,12},{12,16},{16,20},{20,24},{24,28},{1,5},{5,9},{9,... | collective-permute-start | bytes 12488 | tf_op jit(solution)/shard_map/ppermute | solution.py:13
  106.0 7.3 %collective-permute-start.17 = (f32[8,1,256]{2,0,1:T(8,128)S(1)}, f32[8,1,256]{2,0,1:T(8,128)S(1)}, u32[]{:S(2)}, u32[]{:S(2)}) collective-permute-start(f32[8,1,256]{2,0,1:T(8,128)S(1)} %get-tuple-element.17), channel_id=1, source_target_pairs={{32,0},{64,32},{96,64},{128,96},{160,128},{192,160},{224,192},{33,... | collective-permute-start | bytes 24584 | tf_op jit(solution)/shard_map/ppermute | solution.py:16
  107.3 7.4 %collective-permute-start.16 = (f32[8,1,256]{2,0,1:T(8,128)S(1)}, f32[8,1,256]{2,0,1:T(8,128)S(1)}, u32[]{:S(2)}, u32[]{:S(2)}) collective-permute-start(f32[8,1,256]{2,0,1:T(8,128)S(1)} %get-tuple-element.18), channel_id=1, source_target_pairs={{0,32},{32,64},{64,96},{96,128},{128,160},{160,192},{192,224},{1,3... | collective-permute-start | bytes 24584 | tf_op jit(solution)/shard_map/ppermute | solution.py:13
  115.3 6.7 %collective-permute-start.18 = (f32[8,130,1]{1,0,2:T(8,128)S(1)}, f32[8,130,1]{1,0,2:T(8,128)S(1)}, u32[]{:S(2)}, u32[]{:S(2)}) collective-permute-start(f32[8,130,1]{1,0,2:T(8,128)S(1)} %copy.25), channel_id=1, source_target_pairs={{0,4},{4,8},{8,12},{12,16},{16,20},{20,24},{24,28},{1,5},{5,9},{9,... | collective-permute-start | bytes 12488 | tf_op jit(solution)/shard_map/ppermute | solution.py:13
  120.5 6.7 %collective-permute-start.19 = (f32[8,130,1]{1,0,2:T(8,128)S(1)}, f32[8,130,1]{1,0,2:T(8,128)S(1)}, u32[]{:S(2)}, u32[]{:S(2)}) collective-permute-start(f32[8,130,1]{1,0,2:T(8,128)S(1)} %copy.27), channel_id=1, source_target_pairs={{4,0},{8,4},{12,8},{16,12},{20,16},{24,20},{28,24},{5,1},{9,5},{13... | collective-permute-start | bytes 12488 | tf_op jit(solution)/shard_map/ppermute | solution.py:16
Sparse Core Ops, SparseCore 0:
  131.8 71.4 all-gather.1
where the time goes:
time: 538 us; the launch traced here: 537 us
  blocking collectives  310 us (58%)
  waiting for transfers between devices  90.3 us (17%)
  starting transfers between devices  62.9 us (12%)
  other arithmetic  22.4 us (4%)
  local copies, waits for them, and re-layouts  20.9 us (4%)
  matrix products  16.7 us (3%)
  between operations  14.3 us (3%)
    psum x1, blocking collectives, shards(): total = lax.psum(partial_gram, ('lx', 'ly'))  310 us
    all_gather x1, waiting for transfers between devices, shards(): lax.all_gather(paired, 'blk', axis=1, tiled=True)  71.7 us
    ppermute x10, starting transfers between devices, extended(): lax.ppermute(lax.slice_in_dim(block, block.shape[dim] - width, None, axis...  49.7 us
    dot_general x1, matrix products, gram_rows(): lax.dot_general(flat, search_flat, (((1,), (1,)), ((), ())), precision=la...  16.7 us
    ppermute x10, starting transfers between devices, extended(): lax.ppermute(lax.slice_in_dim(block, 0, width, axis=dim), axis, backward)  13.1 us
  transfers between devices with their start and end apart: 21, of which 11 were waited for; matrix products, arithmetic and copies ran while one was open for 1% of the time, Pallas kernels for 0%

commit v1 on v0

--- a/solution.py
+++ b/solution.py
@@ -3,6 +3,13 @@
 import jax.numpy as jnp
 from jax import lax
 from jax.sharding import PartitionSpec as P
+
+
+def swapped_in(x, axis, dim):
+    size = lax.axis_size(axis)
+    tiles = jnp.stack([x for _ in range(size)])
+    tiles = lax.all_to_all(tiles, axis, split_axis=0, concat_axis=0)
+    return jnp.concatenate(tiles, axis=dim)
 
 
 def extended(block, sides, width):
@@ -63,7 +70,7 @@
     padded_field = extended(filtered, (("lx", 1), ("ly", 2)), 1)
     image = scaled_step(padded_field, onsite_energy, present)
     paired = jnp.stack([filtered, image])
-    partial_gram = gram_rows(lax.all_gather(paired, "blk", axis=1, tiled=True), search_vectors)
+    partial_gram = gram_rows(swapped_in(paired, "blk", 1), search_vectors)
     total = lax.psum(partial_gram, ("lx", "ly"))
     return total * scale_factor
 

time: 538 us -> 555 us (1.032)
  local copies, waits for them, and re-layouts: 20.9 us -> 40.1 us
  between operations: 14.3 us -> 0.97 us
  waiting for transfers between devices: 90.3 us -> 101 us
  matrix products: 16.7 us -> 6.76 us
  starting transfers between devices: 62.9 us -> 69.1 us
    all_to_all x0 -> x1, waiting for transfers between devices: none -> 82.1 us  [swapped_in(): tiles = lax.all_to_all(tiles, axis, split_axis=0, concat_axis=0)]
    all_gather x1 -> x0, waiting for transfers between devices: 71.7 us -> none  [shards(): lax.all_gather(paired, 'blk', axis=1, tiled=True)]
    reshape x0 -> x2, local copies, waits for them, and re-layouts: none -> 13.6 us  [the longest x1 9.45 us: gram_rows(): search_flat = search_vectors.reshape(search_vectors.shape[0], nrows * ncols)]
    dot_general x1, matrix products: 16.7 us -> 6.76 us  [gram_rows(): lax.dot_general(flat, search_flat, (((1,), (1,)), ((), ())), precision=la...]
    all_to_all x0 -> x1, starting transfers between devices: none -> 6.24 us  [swapped_in(): tiles = lax.all_to_all(tiles, axis, split_axis=0, concat_axis=0)]
  transfers between devices with their start and end apart: 21 -> 21, of which waited for: 11 -> 11; matrix products, arithmetic and copies ran while one was open for 1% -> 3% of each run, Pallas kernels for 0% -> 0%
where the time goes in v1:
time: 555 us; the launch traced here: 553 us
  blocking collectives  314 us (57%)
  waiting for transfers between devices  101 us (18%)
  starting transfers between devices  69.1 us (12%)
  local copies, waits for them, and re-layouts  40.1 us (7%)
  other arithmetic  21 us (4%)
  matrix products  6.76 us (1%)
    psum x1, blocking collectives, shards(): total = lax.psum(partial_gram, ('lx', 'ly'))  314 us
    all_to_all x1, waiting for transfers between devices, swapped_in(): tiles = lax.all_to_all(tiles, axis, split_axis=0, concat_axis=0)  82.1 us
    ppermute x10, starting transfers between devices, extended(): lax.ppermute(lax.slice_in_dim(block, block.shape[dim] - width, None, axis...  49.7 us
    ppermute x10, starting transfers between devices, extended(): lax.ppermute(lax.slice_in_dim(block, 0, width, axis=dim), axis, backward)  13.1 us
  transfers between devices with their start and end apart: 21, of which 11 were waited for; matrix products, arithmetic and copies ran while one was open for 3% of the time, Pallas kernels for 0%

profile of v1, /device:TPU:16, one launch (start us, length us, event | category | flops | bytes accessed | tf_op | source)
XLA Modules:
  0.0 553.0 jit_solution(11055479898664694594)
XLA Ops:
  0.9 1.8 copy_multiply_fusion
  2.8 1.3 collective-permute-start.1
  4.1 4.5 collective-permute-start
  8.6 1.3 collective-permute-done
  11.0 1.3 collective-permute-start.3
  12.3 4.5 collective-permute-start.2
  16.9 1.3 collective-permute-done.2
  18.2 1.2 copy.15
  20.5 1.9 broadcast_multiply_fusion
  22.5 1.3 collective-permute-start.5
  23.8 4.8 collective-permute-start.4
  28.6 1.3 collective-permute-done.4
  31.1 1.4 copy.18
  32.8 1.3 collective-permute-start.7
  34.1 4.8 collective-permute-start.6
  40.3 1.2 copy.19
  41.5 1.2 copy.21
  42.6 2.6 fusion.28
  45.3 1.3 collective-permute-start.9
  46.6 4.8 collective-permute-start.8
  51.4 1.3 collective-permute-done.8
  53.8 1.4 copy.22
  55.2 5.0 collective-permute-start.10
  60.6 1.3 collective-permute-start.11
  62.3 5.0 collective-permute-done.11
  68.5 1.8 fusion.21
  70.3 1.3 collective-permute-start.13
  71.6 4.9 collective-permute-start.12
  76.5 1.3 collective-permute-done.12
  78.9 1.4 copy.26
  80.7 1.3 collective-permute-start.15
  82.0 5.4 collective-permute-start.14
  91.1 8.3 %fusion.14 = f32[8,128,256]{2,0,1:T(8,128)S(1)} fusion(f32[8,128,256]{2,0,1:T(8,128)S(1)} %fusion.28, f32[8,128,256]{2,0,1:T(8,128)} %copy-done.1, f32[8,1,256]{2,0,1:T(8,128)S(1)} %collective-permute-done.12, f32[8,1,256]{2,0,1:T(8,128)S(1)} %collective-permute-done.13, f32[8,130,1]{2,0,1:T(8,128)} %copy.29, f32[8,130,1]{2,0,1:T(8,128)} %copy.27, ...), kind=kLoop, calls=%fused_computation.29 | loop fusion | flops 6815744 | bytes 5562516 | tf_op jit(solution)/shard_map/add | solution.py:67
  99.5 1.3 collective-permute-start.17
  100.8 6.0 %collective-permute-start.16 = (f32[8,1,256]{2,0,1:T(8,128)S(1)}, f32[8,1,256]{2,0,1:T(8,128)S(1)}, u32[]{:S(2)}, u32[]{:S(2)}) collective-permute-start(f32[8,1,256]{2,0,1:T(8,128)S(1)} %get-tuple-element.18), channel_id=1, source_target_pairs={{0,32},{32,64},{64,96},{96,128},{128,160},{160,192},{192,224},{1,3... | collective-permute-start | bytes 24584 | tf_op jit(solution)/shard_map/ppermute | solution.py:20
  106.8 1.3 collective-permute-done.16
  108.8 4.8 collective-permute-start.18
  114.0 1.5 collective-permute-start.19
  115.9 4.8 collective-permute-done.19
  121.9 1.8 fusion.5
  123.8 4.0 stack.19
  127.8 6.2 %all-to-all-start = ((f32[4,2,8,128,256]{4,2,3,1,0:T(8,128)}), f32[4,2,8,128,256]{4,2,3,1,0:T(8,128)}, u32[]{:S(2)}, u32[]{:S(2)}) async-start(f32[4,2,8,128,256]{4,2,3,1,0:T(8,128)} %stack.19), calls=%async_computation | async-start | bytes 16777216 | tf_op jit(solution)/shard_map/all_to_all | solution.py:11
  134.0 9.5 %reshape.17 = f32[64,32768,1]{1,0,2:T(8,128)} reshape(f32[64,128,256]{2,1,0:T(8,128)} %param.6) | data formatting | bytes 16777216 | tf_op jit(solution)/shard_map/reshape | solution.py:45
  143.4 82.1 %all-to-all-done = f32[4,2,8,128,256]{4,2,3,1,0:T(8,128)} async-done(((f32[4,2,8,128,256]{4,2,3,1,0:T(8,128)}), f32[4,2,8,128,256]{4,2,3,1,0:T(8,128)}, u32[]{:S(2)}, u32[]{:S(2)}) %all-to-all-start) | async-done | bytes 8388640 | tf_op jit(solution)/shard_map/all_to_all | solution.py:11
  225.5 4.1 copy.34
  229.7 1.7 copy-done
  231.3 6.8 %fusion.52 = f32[2,32,64]{2,1,0:T(8,128)S(1)} fusion(f32[2,32,32768]{2,1,0:T(8,128)S(1)} %bitcast.12, f32[64,32768,1]{1,0,2:T(8,128)S(1)} %copy-done), kind=kOutput, calls=%fused_computation.104 | convolution fusion | flops 1610612736 | bytes 16793600 | tf_op jit(solution)/shard_map/dot_general | solution.py:46
  238.1 314.3 %psum.7 = f32[2,32,64]{2,1,0:T(8,128)S(1)} all-reduce(f32[2,32,64]{2,1,0:T(8,128)S(1)} %fusion.52), channel_id=1, replica_groups=mesh['lx'=8,'ly'=8,'blk'=4] {'lx','ly'}, use_global_device_ids=true, to_apply=%region_0.1 | all-reduce | flops 4096 | bytes 32768 | tf_op jit(solution)/shard_map/psum | solution.py:74
  (54 shorter events, 16.8 us)
Async XLA Ops:
  2.8 5.9 %collective-permute-start.1 = (f32[8,1,256]{2,0,1:T(8,128)S(1)}, f32[8,1,256]{2,0,1:T(8,128)S(1)}, u32[]{:S(2)}, u32[]{:S(2)}) collective-permute-start(f32[8,1,256]{2,0,1:T(8,128)S(1)} %get-tuple-element.25), channel_id=1, source_target_pairs={{32,0},{64,32},{96,64},{128,96},{160,128},{192,160},{224,192},{33,... | collective-permute-start | bytes 24584 | tf_op jit(solution)/shard_map/ppermute | solution.py:23
  4.1 5.9 %collective-permute-start = (f32[8,1,256]{2,0,1:T(8,128)S(1)}, f32[8,1,256]{2,0,1:T(8,128)S(1)}, u32[]{:S(2)}, u32[]{:S(2)}) collective-permute-start(f32[8,1,256]{2,0,1:T(8,128)S(1)} %get-tuple-element.26), channel_id=1, source_target_pairs={{0,32},{32,64},{64,96},{96,128},{128,160},{160,192},{192,224},{1,3... | collective-permute-start | bytes 24584 | tf_op jit(solution)/shard_map/ppermute | solution.py:20
  10.3 10.3 %copy-start.2 = (f32[128,256]{1,0:T(8,128)S(1)}, f32[128,256]{1,0:T(8,128)}, u32[]{:S(2)}) copy-start(f32[128,256]{1,0:T(8,128)} %param.7) | copy-start | bytes 393220
  11.0 8.4 %collective-permute-start.3 = (f32[8,130,1]{1,0,2:T(8,128)S(1)}, f32[8,130,1]{1,0,2:T(8,128)S(1)}, u32[]{:S(2)}, u32[]{:S(2)}) collective-permute-start(f32[8,130,1]{1,0,2:T(8,128)S(1)} %copy.16), channel_id=1, source_target_pairs={{4,0},{8,4},{12,8},{16,12},{20,16},{24,20},{28,24},{5,1},{9,5},{13... | collective-permute-start | bytes 12488 | tf_op jit(solution)/shard_map/ppermute | solution.py:23
  12.3 5.9 %collective-permute-start.2 = (f32[8,130,1]{1,0,2:T(8,128)S(1)}, f32[8,130,1]{1,0,2:T(8,128)S(1)}, u32[]{:S(2)}, u32[]{:S(2)}) collective-permute-start(f32[8,130,1]{1,0,2:T(8,128)S(1)} %copy.14), channel_id=1, source_target_pairs={{0,4},{4,8},{8,12},{12,16},{16,20},{20,24},{24,28},{1,5},{5,9},{9,... | collective-permute-start | bytes 12488 | tf_op jit(solution)/shard_map/ppermute | solution.py:20
  22.5 6.1 %collective-permute-start.5 = (f32[8,1,256]{2,0,1:T(8,128)S(1)}, f32[8,1,256]{2,0,1:T(8,128)S(1)}, u32[]{:S(2)}, u32[]{:S(2)}) collective-permute-start(f32[8,1,256]{2,0,1:T(8,128)S(1)} %get-tuple-element.23), channel_id=1, source_target_pairs={{32,0},{64,32},{96,64},{128,96},{160,128},{192,160},{224,192},{33,... | collective-permute-start | bytes 24584 | tf_op jit(solution)/shard_map/ppermute | solution.py:23
  23.8 6.2 %collective-permute-start.4 = (f32[8,1,256]{2,0,1:T(8,128)S(1)}, f32[8,1,256]{2,0,1:T(8,128)S(1)}, u32[]{:S(2)}, u32[]{:S(2)}) collective-permute-start(f32[8,1,256]{2,0,1:T(8,128)S(1)} %get-tuple-element.24), channel_id=1, source_target_pairs={{0,32},{32,64},{64,96},{96,128},{128,160},{160,192},{192,224},{1,3... | collective-permute-start | bytes 24584 | tf_op jit(solution)/shard_map/ppermute | solution.py:20
  32.8 8.7 %collective-permute-start.7 = (f32[8,130,1]{1,0,2:T(8,128)S(1)}, f32[8,130,1]{1,0,2:T(8,128)S(1)}, u32[]{:S(2)}, u32[]{:S(2)}) collective-permute-start(f32[8,130,1]{1,0,2:T(8,128)S(1)} %copy.20), channel_id=1, source_target_pairs={{4,0},{8,4},{12,8},{16,12},{20,16},{24,20},{28,24},{5,1},{9,5},{13... | collective-permute-start | bytes 12488 | tf_op jit(solution)/shard_map/ppermute | solution.py:23
  34.1 6.2 %collective-permute-start.6 = (f32[8,130,1]{1,0,2:T(8,128)S(1)}, f32[8,130,1]{1,0,2:T(8,128)S(1)}, u32[]{:S(2)}, u32[]{:S(2)}) collective-permute-start(f32[8,130,1]{1,0,2:T(8,128)S(1)} %copy.18), channel_id=1, source_target_pairs={{0,4},{4,8},{8,12},{12,16},{16,20},{20,24},{24,28},{1,5},{5,9},{9,... | collective-permute-start | bytes 12488 | tf_op jit(solution)/shard_map/ppermute | solution.py:20
  45.3 6.1 %collective-permute-start.9 = (f32[8,1,256]{2,0,1:T(8,128)S(1)}, f32[8,1,256]{2,0,1:T(8,128)S(1)}, u32[]{:S(2)}, u32[]{:S(2)}) collective-permute-start(f32[8,1,256]{2,0,1:T(8,128)S(1)} %get-tuple-element.21), channel_id=1, source_target_pairs={{32,0},{64,32},{96,64},{128,96},{160,128},{192,160},{224,192},{33,... | collective-permute-start | bytes 24584 | tf_op jit(solution)/shard_map/ppermute | solution.py:23
  46.6 6.2 %collective-permute-start.8 = (f32[8,1,256]{2,0,1:T(8,128)S(1)}, f32[8,1,256]{2,0,1:T(8,128)S(1)}, u32[]{:S(2)}, u32[]{:S(2)}) collective-permute-start(f32[8,1,256]{2,0,1:T(8,128)S(1)} %get-tuple-element.22), channel_id=1, source_target_pairs={{0,32},{32,64},{64,96},{96,128},{128,160},{160,192},{192,224},{1,3... | collective-permute-start | bytes 24584 | tf_op jit(solution)/shard_map/ppermute | solution.py:20
  55.2 6.6 %collective-permute-start.10 = (f32[8,130,1]{1,0,2:T(8,128)S(1)}, f32[8,130,1]{1,0,2:T(8,128)S(1)}, u32[]{:S(2)}, u32[]{:S(2)}) collective-permute-start(f32[8,130,1]{1,0,2:T(8,128)S(1)} %copy.22), channel_id=1, source_target_pairs={{0,4},{4,8},{8,12},{12,16},{16,20},{20,24},{24,28},{1,5},{5,9},{9,... | collective-permute-start | bytes 12488 | tf_op jit(solution)/shard_map/ppermute | solution.py:20
  60.6 6.7 %collective-permute-start.11 = (f32[8,130,1]{1,0,2:T(8,128)S(1)}, f32[8,130,1]{1,0,2:T(8,128)S(1)}, u32[]{:S(2)}, u32[]{:S(2)}) collective-permute-start(f32[8,130,1]{1,0,2:T(8,128)S(1)} %copy.24), channel_id=1, source_target_pairs={{4,0},{8,4},{12,8},{16,12},{20,16},{24,20},{28,24},{5,1},{9,5},{13... | collective-permute-start | bytes 12488 | tf_op jit(solution)/shard_map/ppermute | solution.py:23
  70.3 7.7 %copy-start.1 = (f32[8,128,256]{2,0,1:T(8,128)}, f32[8,128,256]{2,0,1:T(8,128)S(1)}, u32[]{:S(2)}) copy-start(f32[8,128,256]{2,0,1:T(8,128)S(1)} %fusion.21) | copy-start | bytes 3145732
  70.3 6.2 %collective-permute-start.13 = (f32[8,1,256]{2,0,1:T(8,128)S(1)}, f32[8,1,256]{2,0,1:T(8,128)S(1)}, u32[]{:S(2)}, u32[]{:S(2)}) collective-permute-start(f32[8,1,256]{2,0,1:T(8,128)S(1)} %get-tuple-element.19), channel_id=1, source_target_pairs={{32,0},{64,32},{96,64},{128,96},{160,128},{192,160},{224,192},{33,... | collective-permute-start | bytes 24584 | tf_op jit(solution)/shard_map/ppermute | solution.py:23
  71.6 6.3 %collective-permute-start.12 = (f32[8,1,256]{2,0,1:T(8,128)S(1)}, f32[8,1,256]{2,0,1:T(8,128)S(1)}, u32[]{:S(2)}, u32[]{:S(2)}) collective-permute-start(f32[8,1,256]{2,0,1:T(8,128)S(1)} %get-tuple-element.20), channel_id=1, source_target_pairs={{0,32},{32,64},{64,96},{96,128},{128,160},{160,192},{192,224},{1,3... | collective-permute-start | bytes 24584 | tf_op jit(solution)/shard_map/ppermute | solution.py:20
  78.9 8.5 %copy-start.3 = (f32[5]{0:T(128)S(1)}, f32[5]{0:T(128)}, u32[]{:S(2)}) copy-start(f32[5]{0:T(128)} %param.9) | copy-start | bytes 64
  80.7 9.3 %collective-permute-start.15 = (f32[8,130,1]{1,0,2:T(8,128)S(1)}, f32[8,130,1]{1,0,2:T(8,128)S(1)}, u32[]{:S(2)}, u32[]{:S(2)}) collective-permute-start(f32[8,130,1]{1,0,2:T(8,128)S(1)} %copy.28), channel_id=1, source_target_pairs={{4,0},{8,4},{12,8},{16,12},{20,16},{24,20},{28,24},{5,1},{9,5},{13... | collective-permute-start | bytes 12488 | tf_op jit(solution)/shard_map/ppermute | solution.py:23
  82.0 6.8 %collective-permute-start.14 = (f32[8,130,1]{1,0,2:T(8,128)S(1)}, f32[8,130,1]{1,0,2:T(8,128)S(1)}, u32[]{:S(2)}, u32[]{:S(2)}) collective-permute-start(f32[8,130,1]{1,0,2:T(8,128)S(1)} %copy.26), channel_id=1, source_target_pairs={{0,4},{4,8},{8,12},{12,16},{16,20},{20,24},{24,28},{1,5},{5,9},{9,... | collective-permute-start | bytes 12488 | tf_op jit(solution)/shard_map/ppermute | solution.py:20
  99.5 7.3 %collective-permute-start.17 = (f32[8,1,256]{2,0,1:T(8,128)S(1)}, f32[8,1,256]{2,0,1:T(8,128)S(1)}, u32[]{:S(2)}, u32[]{:S(2)}) collective-permute-start(f32[8,1,256]{2,0,1:T(8,128)S(1)} %get-tuple-element.17), channel_id=1, source_target_pairs={{32,0},{64,32},{96,64},{128,96},{160,128},{192,160},{224,192},{33,... | collective-permute-start | bytes 24584 | tf_op jit(solution)/shard_map/ppermute | solution.py:23
  100.8 7.4 %collective-permute-start.16 = (f32[8,1,256]{2,0,1:T(8,128)S(1)}, f32[8,1,256]{2,0,1:T(8,128)S(1)}, u32[]{:S(2)}, u32[]{:S(2)}) collective-permute-start(f32[8,1,256]{2,0,1:T(8,128)S(1)} %get-tuple-element.18), channel_id=1, source_target_pairs={{0,32},{32,64},{64,96},{96,128},{128,160},{160,192},{192,224},{1,3... | collective-permute-start | bytes 24584 | tf_op jit(solution)/shard_map/ppermute | solution.py:20
  108.8 6.7 %collective-permute-start.18 = (f32[8,130,1]{1,0,2:T(8,128)S(1)}, f32[8,130,1]{1,0,2:T(8,128)S(1)}, u32[]{:S(2)}, u32[]{:S(2)}) collective-permute-start(f32[8,130,1]{1,0,2:T(8,128)S(1)} %copy.30), channel_id=1, source_target_pairs={{0,4},{4,8},{8,12},{12,16},{16,20},{20,24},{24,28},{1,5},{5,9},{9,... | collective-permute-start | bytes 12488 | tf_op jit(solution)/shard_map/ppermute | solution.py:20
  114.0 6.7 %collective-permute-start.19 = (f32[8,130,1]{1,0,2:T(8,128)S(1)}, f32[8,130,1]{1,0,2:T(8,128)S(1)}, u32[]{:S(2)}, u32[]{:S(2)}) collective-permute-start(f32[8,130,1]{1,0,2:T(8,128)S(1)} %copy.32), channel_id=1, source_target_pairs={{4,0},{8,4},{12,8},{16,12},{20,16},{24,20},{28,24},{5,1},{9,5},{13... | collective-permute-start | bytes 12488 | tf_op jit(solution)/shard_map/ppermute | solution.py:23
  127.8 97.8 %all-to-all-start = ((f32[4,2,8,128,256]{4,2,3,1,0:T(8,128)}), f32[4,2,8,128,256]{4,2,3,1,0:T(8,128)}, u32[]{:S(2)}, u32[]{:S(2)}) async-start(f32[4,2,8,128,256]{4,2,3,1,0:T(8,128)} %stack.19), calls=%async_computation | async-start | bytes 16777216 | tf_op jit(solution)/shard_map/all_to_all | solution.py:11
  225.5 5.8 %copy-start = (f32[64,32768,1]{1,0,2:T(8,128)S(1)}, f32[64,32768,1]{1,0,2:T(8,128)}, u32[]{:S(2)}) copy-start(f32[64,32768,1]{1,0,2:T(8,128)} %reshape.17) | copy-start | bytes 25165828
